TPU v7x, 32 devices: a whole 2x2x4 slice. The times are simulated.
32 devices in a mesh: tower: 2 (over x), dp: 16 (over z, y, core).
Axes of the slice: x: 2, y: 2, z: 4, core: 2. Of those that a mesh axis runs over, the one named last changes fastest.
Arguments:
- tokens: bfloat16 [2, 16384, 768], P('tower', 'dp'), may hold values from -6 to 6
- segments: int32 [2, 128, 128], P('tower', 'dp'), may hold values from 0 to 7, as said below
- pairs: int32 [1024], replicated, may hold values from 0 to 1023, as said below
- scores: float32 [1024], replicated, may hold values from -0.5 to 1
- w_qkv: bfloat16 [768, 2304], replicated, may hold values from -0.21875 to 0.21875
- b_query: float32 [768], replicated, may hold values from -1.75 to 1.75
- b_value: float32 [768], replicated, may hold values from -3 to 3
- w_out: bfloat16 [768, 768], replicated, may hold values from -0.4375 to 0.4375
- b_out: float32 [768], replicated, may hold values from -3 to 3
- gain_one: float32 [768], replicated, may hold values from 0.25 to 1.75
- shift_one: float32 [768], replicated, may hold values from -1.25 to 1.25
- w_in: bfloat16 [768, 3072], replicated, may hold values from -0.21875 to 0.21875
- b_in: float32 [3072], replicated, may hold values from -3 to 3
- w_down: bfloat16 [3072, 768], replicated, may hold values from -0.109375 to 0.109375
- b_down: float32 [768], replicated, may hold values from -3 to 3
- gain_two: float32 [768], replicated, may hold values from 0.25 to 1.75
- shift_two: float32 [768], replicated, may hold values from -0.625 to 0.625
Outputs:
- output_rows: bfloat16 [2, 16384, 768], P('tower', 'dp')
- grad_tokens: float32 [2, 16384, 768], P('tower', 'dp')
- grad_w_qkv: float32 [768, 2304], replicated
- grad_b_query: float32 [768], replicated
- grad_b_value: float32 [768], replicated
- grad_w_out: float32 [768, 768], replicated
- grad_b_out: float32 [768], replicated
- grad_gain_one: float32 [768], replicated
- grad_shift_one: float32 [768], replicated
- grad_w_in: float32 [768, 3072], replicated
- grad_b_in: float32 [3072], replicated
- grad_w_down: float32 [3072, 768], replicated
- grad_b_down: float32 [768], replicated
- grad_gain_two: float32 [768], replicated
- grad_shift_two: float32 [768], replicated
Inputs may be any that keep to these rules, and one draw needn't show every extreme that they name: `segments`: within each packed row the numbers never fall along the row and run from 0 to 7, each one present. `pairs`: every B sentence is the partner of exactly one A sentence.
All inputs are finite; a program needn't handle non-finite values.
Results may differ from a plain program's by a relative error of at most 0.008.
Values may be sent and summed in bfloat16 or wider, within the bound.
No kernel may reach another device: no remote copies, remote signals or barrier semaphores. Data moves between devices by JAX's collectives and lax.ppermute only.
A program may use at most 256 MiB of HBM per device.

v0:
```python
import math
import jax
import jax.numpy as jnp
from jax import lax
from jax.sharding import PartitionSpec as P

HEADS = 12
SEG_ROW = 8
loss_scale = 65536.0


def gelu_exact(values_in):
    return jax.nn.gelu(values_in, approximate=False)


def layer_norm(values_in, gain_vec, shift_vec):
    row_mean = jnp.mean(values_in, -1, keepdims=True)
    centered = values_in - row_mean
    inv_std = lax.rsqrt(jnp.mean(centered * centered, -1, keepdims=True) + 1e-12)
    normed = centered * inv_std
    return (normed * gain_vec + shift_vec, normed, inv_std)


def norm_back(gradient, normed, inv_std, gain_vec):
    scaled = gradient * gain_vec
    inner = (
        scaled
        - jnp.mean(scaled, -1, keepdims=True)
        - normed * jnp.mean(scaled * normed, -1, keepdims=True)
    )
    return (inner * inv_std, jnp.sum(gradient * normed, 0), jnp.sum(gradient, 0))


def on_device(
    tokens,
    segments,
    pairs,
    scores,
    w_qkv,
    b_query,
    b_value,
    w_out,
    b_out,
    gain_one,
    shift_one,
    w_in,
    b_in,
    w_down,
    b_down,
    gain_two,
    shift_two,
):
    f32 = jnp.float32
    bf16 = jnp.bfloat16
    flat_rows = tokens[0]
    seg_rows = segments[0]
    row_count = seg_rows.shape[0]
    row_len = seg_rows.shape[1]
    model_width = flat_rows.shape[1]
    token_count = flat_rows.shape[0]
    head_dim = model_width // HEADS
    head_shape = (row_count, row_len, HEADS, head_dim)
    score_scale = 1.0 / math.sqrt(head_dim)
    joint_rows = jnp.dot(flat_rows, w_qkv, preferred_element_type=f32)
    query_rows = (joint_rows[:, :model_width] + b_query).astype(bf16).reshape(head_shape)
    key_rows = joint_rows[:, model_width : 2 * model_width].astype(bf16).reshape(head_shape)
    value_rows = (joint_rows[:, 2 * model_width :] + b_value).astype(bf16).reshape(head_shape)
    same_segment = (seg_rows[:, :, None] == seg_rows[:, None, :])[:, None]

    def score_of():
        raw = (
            jnp.einsum("rqhd,rkhd->rhqk", query_rows, key_rows, preferred_element_type=f32)
            * score_scale
        )
        return jnp.where(same_segment, raw, -1e30)

    scores_now = score_of()
    row_max = jnp.max(scores_now, -1, keepdims=True)
    expo = jnp.exp(scores_now - row_max)
    denom = jnp.sum(expo, -1, keepdims=True)
    log_total = row_max + jnp.log(denom)
    attn_low = (expo / denom).astype(bf16)
    context = jnp.einsum("rhqk,rkhd->rqhd", attn_low, value_rows, preferred_element_type=f32)
    context = context.astype(bf16).reshape(token_count, model_width)
    attended = jnp.dot(context, w_out, preferred_element_type=f32) + b_out
    hidden, normed_one, inv_std_one = layer_norm(
        flat_rows.astype(f32) + attended, gain_one, shift_one
    )
    hidden_low = hidden.astype(bf16)
    up_rows = jnp.dot(hidden_low, w_in, preferred_element_type=f32) + b_in
    gelu_value, gelu_back = jax.vjp(gelu_exact, up_rows)
    activated = gelu_value.astype(bf16)
    down_rows = jnp.dot(activated, w_down, preferred_element_type=f32) + b_down
    output_rows, normed_two, inv_std_two = layer_norm(hidden + down_rows, gain_two, shift_two)
    onehot = (seg_rows[:, :, None] == jnp.arange(SEG_ROW, dtype=jnp.int32)[None, None, :]).astype(
        f32
    )
    counts = jnp.sum(onehot, 1)
    seg_sums = jnp.einsum(
        "rts,rtd->rsd",
        onehot,
        output_rows.reshape(row_count, row_len, model_width),
        precision=lax.Precision.HIGHEST,
    )
    seg_count = row_count * SEG_ROW
    pooled_low = (seg_sums / counts[:, :, None]).reshape(seg_count, model_width).astype(bf16)
    tower_index = lax.axis_index("tower")
    row_block = lax.axis_index("dp")
    pair_count = pairs.shape[0]
    everyone = lax.all_gather(pooled_low, ("tower", "dp"), axis=0, tiled=True)
    other_side = lax.dynamic_slice_in_dim(everyone, (1 - tower_index) * pair_count, pair_count, 0)
    own_index = row_block * seg_count + jnp.arange(seg_count, dtype=jnp.int32)
    inverse = (
        jnp.zeros((pair_count,), jnp.int32).at[pairs].set(jnp.arange(pair_count, dtype=jnp.int32))
    )
    back_pick = inverse[own_index]
    partner_index = jnp.where(tower_index == 0, pairs[own_index], back_pick)
    target_index = jnp.where(tower_index == 0, own_index, back_pick)
    partner = other_side[partner_index].astype(f32)
    target = scores[target_index]
    mine = pooled_low.astype(f32)
    inv_mine = lax.rsqrt(jnp.sum(mine * mine, -1) + 1e-06)
    inv_partner = lax.rsqrt(jnp.sum(partner * partner, -1) + 1e-06)
    cosine = jnp.sum(mine * partner, -1) * inv_mine * inv_partner
    coeff = loss_scale * 2.0 * (cosine - target) / pair_count
    d_pooled = coeff[:, None] * (
        partner * (inv_mine * inv_partner)[:, None] - (cosine * inv_mine * inv_mine)[:, None] * mine
    )
    per_token = d_pooled.reshape(row_count, SEG_ROW, model_width) / counts[:, :, None]
    d_output = jnp.einsum(
        "rts,rsd->rtd", onehot, per_token, precision=lax.Precision.HIGHEST
    ).reshape(token_count, model_width)
    d_mid, grad_gain_two, grad_shift_two = norm_back(d_output, normed_two, inv_std_two, gain_two)
    grad_b_down = jnp.sum(d_mid, 0)
    d_mid_low = d_mid.astype(bf16)
    grad_w_down = jnp.einsum("nf,nd->fd", activated, d_mid_low, preferred_element_type=f32)
    d_act = jnp.einsum("nd,fd->nf", d_mid_low, w_down, preferred_element_type=f32)
    d_up = gelu_back(d_act)[0]
    grad_b_in = jnp.sum(d_up, 0)
    d_up_low = d_up.astype(bf16)
    grad_w_in = jnp.einsum("nd,nf->df", hidden_low, d_up_low, preferred_element_type=f32)
    d_hidden = d_mid + jnp.einsum("nf,df->nd", d_up_low, w_in, preferred_element_type=f32)
    d_first, grad_gain_one, grad_shift_one = norm_back(d_hidden, normed_one, inv_std_one, gain_one)
    grad_b_out = jnp.sum(d_first, 0)
    d_first_low = d_first.astype(bf16)
    grad_w_out = jnp.einsum("nc,nd->cd", context, d_first_low, preferred_element_type=f32)
    d_context = jnp.einsum("nd,cd->nc", d_first_low, w_out, preferred_element_type=f32)
    d_context = d_context.astype(bf16).reshape(head_shape)
    attn_again = jnp.exp(score_of() - log_total)
    attn_again_low = attn_again.astype(bf16)
    d_values = jnp.einsum("rhqk,rqhd->rkhd", attn_again_low, d_context, preferred_element_type=f32)
    d_attn = jnp.einsum("rqhd,rkhd->rhqk", d_context, value_rows, preferred_element_type=f32)
    d_scores = attn_again * (d_attn - jnp.sum(attn_again * d_attn, -1, keepdims=True))
    d_scores_low = d_scores.astype(bf16)
    d_query = (
        jnp.einsum("rhqk,rkhd->rqhd", d_scores_low, key_rows, preferred_element_type=f32)
        * score_scale
    )
    d_keys = (
        jnp.einsum("rhqk,rqhd->rkhd", d_scores_low, query_rows, preferred_element_type=f32)
        * score_scale
    )
    d_query = d_query.reshape(token_count, model_width)
    d_keys = d_keys.reshape(token_count, model_width)
    d_values = d_values.reshape(token_count, model_width)
    grad_b_query = jnp.sum(d_query, 0)
    grad_b_value = jnp.sum(d_values, 0)
    d_joint = jnp.concatenate([d_query, d_keys, d_values], -1).astype(bf16)
    grad_w_qkv = jnp.einsum("nd,ne->de", flat_rows, d_joint, preferred_element_type=f32)
    grad_tokens = d_first + jnp.einsum("ne,de->nd", d_joint, w_qkv, preferred_element_type=f32)
    (
        grad_w_qkv,
        grad_b_query,
        grad_b_value,
        grad_w_out,
        grad_b_out,
        grad_gain_one,
        grad_shift_one,
        grad_w_in,
        grad_b_in,
        grad_w_down,
        grad_b_down,
        grad_gain_two,
        grad_shift_two,
    ) = lax.psum(
        (
            grad_w_qkv,
            grad_b_query,
            grad_b_value,
            grad_w_out,
            grad_b_out,
            grad_gain_one,
            grad_shift_one,
            grad_w_in,
            grad_b_in,
            grad_w_down,
            grad_b_down,
            grad_gain_two,
            grad_shift_two,
        ),
        ("tower", "dp"),
    )
    return (
        output_rows.astype(bf16)[None],
        grad_tokens[None],
        grad_w_qkv,
        grad_b_query,
        grad_b_value,
        grad_w_out,
        grad_b_out,
        grad_gain_one,
        grad_shift_one,
        grad_w_in,
        grad_b_in,
        grad_w_down,
        grad_b_down,
        grad_gain_two,
        grad_shift_two,
    )


def solution(mesh):
    return jax.shard_map(
        on_device,
        mesh=mesh,
        in_specs=(
            P("tower", "dp", None),
            P("tower", "dp", None),
            P(),
            P(),
            P(),
            P(),
            P(),
            P(),
            P(),
            P(),
            P(),
            P(),
            P(),
            P(),
            P(),
            P(),
            P(),
        ),
        out_specs=(
            P("tower", "dp", None),
            P("tower", "dp", None),
            P(),
            P(),
            P(),
            P(),
            P(),
            P(),
            P(),
            P(),
            P(),
            P(),
            P(),
            P(),
            P(),
        ),
        check_vma=False,
    )
```

profile of v0, /device:TPU:0, one launch (start us, length us, event | category | flops | bytes accessed | tf_op | source)
XLA Modules:
  0.0 731.7 jit_solution(16902538640138594596)
XLA Ops:
  7.2 1.5 convert_reduce_fusion
  8.8 1.6 broadcast_compare_fusion
  10.4 5.2 fusion.28
  15.6 1.3 slice.31
  16.9 2.3 fusion.11
  19.2 2.8 copy.45
  22.1 3.1 copy.70
  25.1 2.6 copy.47
  27.7 3.0 copy.72
  30.7 2.6 copy.46
  33.3 2.0 copy.71
  35.3 1.5 fusion.78
  36.9 1.6 fusion.6
  39.6 1.3 fusion.30
  40.9 1.2 copy.52
  42.6 1.7 fusion.79
  45.0 1.9 copy-done.28
  47.0 35.3 %multiply_convert_fusion = (bf16[1024,3072]{1,0:T(8,128)(2,1)S(1)}, f32[1024,3072]{1,0:T(8,128)}, f32[1024,3072]{1,0:T(8,128)}) fusion(f32[3072]{0:T(1024)S(1)} %copy-done.46, bf16[768,3072]{1,0:T(8,128)(2,1)S(1)} %bitcast.168, f32[1024,768]{1,0:T(8,128)S(1)} %get-tuple-element.86, f32[768]{0:T(1024)S(1)} %copy-done.34, f32[768]{0:T(1024)S(1)} %copy-done.28, ...), kind=kOutput, calls=%fused_computation.8 | convolution fusion | flops 5043388416 | bytes 39348224 | tf_op jit(solution)/shard_map/dot_general | solution.py:90
  82.3 5.4 fusion.80
  88.6 1.7 convert_bitcast_fusion
  90.4 1.8 fusion.44
  92.9 1.4 gather_fusion
  95.4 4.6 scatter_custom_fusion
  100.0 1.4 gather_fusion.1
  103.2 1.4 gather_fusion.3
  104.6 1.3 gather.24
  105.9 1.3 pad_clamp_fusion.1
  107.1 1.5 log_add_fusion
  108.7 45.4 %all-gather.2.cloned.1.call-done = bf16[2048,768]{1,0:T(8,128)(2,1)} async-done(((bf16[64,768]{1,0:T(8,128)(2,1)}), bf16[2048,768]{1,0:T(8,128)(2,1)}) %all-gather.2.cloned.1.call-update) | async-done | bytes 3145744 | tf_op jit(solution)/shard_map/all_gather | solution.py:110
  154.1 2.7 constant_dynamic-slice_fusion
  156.7 3.1 gather_fusion.2
  160.9 1.7 fusion.57
  163.0 1.3 rsqrt.49
  165.3 3.4 fusion.74
  168.7 1.5 fusion.12
  170.2 2.0 fusion.75
  172.2 7.7 %fusion.47 = f32[3072,768]{1,0:T(8,128)} fusion(bf16[1024,3072]{1,0:T(8,128)(2,1)S(1)} %bitcast.170, f32[1024,768]{1,0:T(8,128)S(1)} %get-tuple-element.69), kind=kOutput, calls=%fused_computation.99 | convolution fusion | flops 4832624640 | bytes 18874368 | tf_op jit(solution)/shard_map/nf,nd->fd/dot_general | solution.py:136
  180.0 19.2 %fusion.81 = (f32[3072]{0:T(1024)}, bf16[1024,3072]{1,0:T(8,128)(2,1)}) fusion(f32[1024,3072]{1,0:T(8,128)} %get-tuple-element.75, bf16[3072,768]{1,0:T(8,128)(2,1)} %param.30, f32[1024,768]{1,0:T(8,128)} %copy-done.16, f32[1024,3072]{1,0:T(8,128)} %get-tuple-element.87, f32[3072]{0:T(1024)S(1)} %copy-done.47), kind=kOutput, calls=%fused_computation.162 | convolution fusion | flops 4882953216 | bytes 39346176 | tf_op jit(solution)/shard_map/nd,fd->nf/dot_general | solution.py:137
  199.2 11.6 %multiply_reduce_fusion.1 = (f32[768]{0:T(1024)}, f32[1024]{0:T(1024)S(1)}, f32[1024]{0:T(1024)S(1)}, f32[768]{0:T(1024)}, f32[1024,768]{1,0:T(8,128)S(1)}) fusion(f32[1024,768]{1,0:T(8,128)} %copy-done.6, f32[1024]{0:T(1024)S(1)} %add_rsqrt_fusion.2, f32[1024]{0:T(1024)S(1)} %broadcast_multiply_fusion.4, f32[768]{0:T(1024)S(1)} %copy-done.29, ...), kind=kOutput, calls=%fused_computation.44 | convolution fusion | flops 4839698432 | bytes 20472832 | tf_op jit(solution)/shard_map/nf,df->nd/dot_general | solution.py:142
  210.8 8.9 %fusion.14 = f32[768,3072]{1,0:T(8,128)} fusion(bf16[1024,3072]{1,0:T(8,128)(2,1)S(1)} %copy-done.8, f32[1024,768]{1,0:T(8,128)S(1)} %copy-done.7, f32[768]{0:T(1024)S(1)} %copy-done.35, f32[768]{0:T(1024)S(1)} %copy-done.29, f32[1024]{0:T(1024)S(1)} %add_rsqrt_fusion.2, f32[1024]{0:T(1024)S(1)} %broadcast_multiply_fusion.4), kind=kOutput, calls=%fused_computation.50 | convolution fusion | flops 4835770368 | bytes 18888704 | tf_op jit(solution)/shard_map/nd,nf->df/dot_general | solution.py:141
  219.7 1.8 fusion.76
  221.5 2.8 fusion.24
  224.3 2.6 convolution_convert_fusion
  226.9 2.6 copy.53
  229.5 1.9 copy.74
  231.4 6.8 bitcast_convert_fusion
  238.2 7.3 %multiply_reduce_fusion = (f32[8,12,128]{2,1,0:T(8,128)S(1)}, f32[8,12,128,128]{2,3,1,0:T(8,128)}) fusion(f32[8,12,128,128]{2,3,1,0:T(8,128)} %copy-done.1, f32[8,12,128]{2,1,0:T(8,128)S(1)} %copy-done.19, bf16[8,128,12,64]{1,0,3,2:T(8,128)(2,1)S(1)} %bitcast.157, bf16[8,128,12,64]{1,0,3,2:T(8,128)(2,1)S(1)} %bitcast.141), kind=kOutput, calls=%fused_computation.23 | convolution fusion | flops 206032896 | bytes 15826944 | tf_op jit(solution)/shard_map/rqhd,rkhd->rhqk/dot_general | solution.py:152
  245.6 4.9 multiply_convert_fusion.1
  250.5 2.3 fusion.31
  252.7 2.7 bitcast_convert_fusion.1
  255.4 1.2 copy.64
  256.6 1.2 copy.61
  257.9 1.2 copy.58
  260.5 2.2 copy-done.20
  262.7 5.8 convolution_bitcast_fusion
  268.6 2.1 bitcast_reduce_fusion
  271.4 2.4 bitcast_reduce_fusion.1
  274.5 41.7 %all-reduce = (f32[768]{0:T(1024)}, f32[768]{0:T(1024)}, f32[768]{0:T(1024)}, f32[768]{0:T(1024)}, f32[768]{0:T(1024)}, /*index=5*/f32[3072]{0:T(1024)}, f32[768]{0:T(1024)}, f32[768]{0:T(1024)}, f32[768]{0:T(1024)}) all-reduce(f32[768]{0:T(1024)} %reduce_sum.226, ...), channel_id=1, replica_groups=mesh['tower'=2,'dp'=16] {'tower','dp'}, use_global_device_ids=true, to_apply=%region_18.19 | all-reduce | flops 9216 | bytes 73728 | tf_op jit(solution)/shard_map/psum | solution.py:185
  316.2 8.5 %add_bitcast_fusion = f32[1,1024,768]{2,1,0:T(8,128)} fusion(f32[1024,768]{1,0:T(8,128)} %copy-done.15, bf16[1024,2304]{0,1:T(8,128)(2,1)} %copy-done.20, bf16[768,2304]{1,0:T(8,128)(2,1)S(1)} %copy-done), kind=kOutput, calls=%fused_computation.45 | convolution fusion | flops 3624665088 | bytes 14548992 | tf_op jit(solution)/shard_map/ne,de->nd/dot_general | solution.py:170
  324.7 376.1 %all-reduce.4.cloned.1.call-done = (f32[768,2304]{0,1:T(8,128)}, f32[768,768]{1,0:T(8,128)}, f32[768,3072]{1,0:T(8,128)}, f32[3072,768]{1,0:T(8,128)}) async-done(((f32[768,2304]{0,1:T(8,128)}, f32[768,768]{1,0:T(8,128)}, f32[768,3072]{1,0:T(8,128)}, f32[3072,768]{1,0:T(8,128)}), (f32[768,2304]{0,1:T(8,128)}, f32[768,768]{1,0:T(8,128)}, f32[768,3072]{1,0:T(8,128)}, ...) | async-done | bytes 28311568 | tf_op jit(solution)/shard_map/psum | solution.py:185
  700.8 8.0 %copy.65 = f32[768,2304]{1,0:T(8,128)} copy(f32[768,2304]{0,1:T(8,128)} %get-tuple-element.64) | data formatting | bytes 14155776
  708.8 3.4 copy.125
  712.1 8.8 %copy.126 = f32[768,3072]{1,0:T(8,128)} copy(f32[768,3072]{1,0:T(8,128)} %get-tuple-element.113) | data formatting | bytes 18874368
  720.9 3.7 copy.127
  (154 shorter events, 11.9 us)
Async XLA Ops:
  7.2 3.2 copy-start
  7.2 146.9 %all-gather.2.cloned.1.call-start = ((), (), s32[]{:S(2)}) async-start(), calls=%async_computation | async-start | bytes 3244032 | tf_op jit(solution)/shard_map/all_gather | solution.py:110
  15.6 1.3 copy-start.39
  15.6 1.3 copy-start.40
  33.3 2.0 copy-start.9
  33.3 2.0 copy-start.23
  35.3 1.5 copy-start.11
  36.8 2.7 copy-start.1
  36.9 2.7 copy-start.21
  36.9 2.7 copy-start.13
  38.5 2.3 copy-start.22
  40.9 1.4 copy-start.42
  40.9 1.7 copy-start.44
  40.9 1.7 copy-start.48
  42.1 2.2 copy-start.17
  42.1 2.9 slice-start.7
  42.6 2.4 slice-start.8
  42.6 39.7 %slice-start.5 = ((s8[4718592]{0:T(1024)(128)(4,1)}), s8[4194304]{0:T(1024)(128)(4,1)S(1)}, s32[]{:S(2)}) async-start(s8[4718592]{0:T(1024)(128)(4,1)} %bitcast.165), calls=%async_computation.7 | async-start | bytes 8388608
  44.3 38.0 %copy-start.6 = (f32[1024,768]{1,0:T(8,128)}, f32[1024,768]{1,0:T(8,128)S(1)}, u32[]{:S(2)}) copy-start(f32[1024,768]{1,0:T(8,128)S(1)} %get-tuple-element.86) | copy-start | bytes 9437188
  44.3 2.6 copy-start.28
  44.4 2.6 copy-start.34
  44.4 2.6 copy-start.46
  47.0 35.3 %slice-start.6 = ((s8[4718592]{0:T(1024)(128)(4,1)}), s8[524288]{0:T(1024)(128)(4,1)S(1)}, s32[]{:S(2)}) async-start(s8[4718592]{0:T(1024)(128)(4,1)} %bitcast.165), calls=%async_computation.8 | async-start | bytes 1048576
  47.0 35.3 %copy-start.49 = (f32[768]{0:T(1024)S(1)}, f32[768]{0:T(1024)}, u32[]{:S(2)}) copy-start(f32[768]{0:T(1024)} %param.31) | copy-start | bytes 9220
  82.3 5.5 copy-start.50
  87.8 2.5 copy-start.4
  87.8 0.7 copy-start.30
  87.8 0.8 copy-start.41
  87.8 2.5 copy-start.26
  88.6 1.8 copy-start.32
  88.6 1.8 copy-start.24
  88.6 1.8 copy-start.36
  90.3 2.5 copy-start.2
  90.3 12.9 %copy-start.3 = (f32[1024]{0:T(1024)S(1)}, f32[1024]{0:T(1024)}, u32[]{:S(2)}) copy-start(f32[1024]{0:T(1024)} %param.20) | copy-start | bytes 12292
  92.2 608.6 %all-reduce.4.cloned.1.call-start = ((), (), s32[]{:S(2)}) async-start(), calls=%async_computation.1 | async-start | bytes 56623104 | tf_op jit(solution)/shard_map/psum | solution.py:185
  101.4 63.9 %copy-start.25 = (s32[1,8,128]{2,1,0:T(8,128)S(1)}, s32[1,8,128]{2,1,0:T(8,128)}, u32[]{:S(2)}) copy-start(s32[1,8,128]{2,1,0:T(8,128)} %param.18) | copy-start | bytes 12292
  108.7 60.0 %copy-start.27 = (f32[1024]{0:T(1024)S(1)}, f32[1024]{0:T(1024)}, u32[]{:S(2)}) copy-start(f32[1024]{0:T(1024)} %copy-done.26) | copy-start | bytes 12292
  164.4 4.3 copy-start.5
  164.4 4.3 copy-start.31
  164.4 4.3 copy-start.33
  168.7 3.6 slice-start.9
  170.2 2.0 slice-start.10
  172.2 7.7 %copy-start.16 = (f32[1024,768]{1,0:T(8,128)}, f32[1024,768]{1,0:T(8,128)S(1)}, u32[]{:S(2)}) copy-start(f32[1024,768]{1,0:T(8,128)S(1)} %get-tuple-element.69) | copy-start | bytes 9437188
  172.2 7.7 %copy-start.47 = (f32[3072]{0:T(1024)S(1)}, f32[3072]{0:T(1024)}, u32[]{:S(2)}) copy-start(f32[3072]{0:T(1024)} %param.29) | copy-start | bytes 36868
  179.9 19.2 %copy-start.29 = (f32[768]{0:T(1024)S(1)}, f32[768]{0:T(1024)}, u32[]{:S(2)}) copy-start(f32[768]{0:T(1024)} %param.26) | copy-start | bytes 9220
  199.2 11.6 %copy-start.7 = (f32[1024,768]{1,0:T(8,128)S(1)}, f32[1024,768]{1,0:T(8,128)}, u32[]{:S(2)}) copy-start(f32[1024,768]{1,0:T(8,128)} %copy-done.6) | copy-start | bytes 9437188
  199.2 11.6 %copy-start.8 = (bf16[1024,3072]{1,0:T(8,128)(2,1)S(1)}, bf16[1024,3072]{1,0:T(8,128)(2,1)}, u32[]{:S(2)}) copy-start(bf16[1024,3072]{1,0:T(8,128)(2,1)} %get-tuple-element.99) | copy-start | bytes 18874372
  199.2 11.6 %copy-start.35 = (f32[768]{0:T(1024)S(1)}, f32[768]{0:T(1024)}, u32[]{:S(2)}) copy-start(f32[768]{0:T(1024)} %param.27) | copy-start | bytes 9220
  219.7 1.8 copy-start.18
  221.5 2.8 copy-start.15
  221.5 2.8 copy-start.45
  229.5 1.9 copy-start.19
  231.4 6.8 copy-start.14
  231.4 14.2 %slice-start = ((s8[6291456]{0:T(1024)(128)(4,1)}), s8[4194304]{0:T(1024)(128)(4,1)S(1)}, s32[]{:S(2)}) async-start(s8[6291456]{0:T(1024)(128)(4,1)} %bitcast.138), calls=%async_computation.2 | async-start | bytes 8388608
  238.2 7.4 %slice-start.1 = ((s8[6291456]{0:T(1024)(128)(4,1)}), s8[2097152]{0:T(1024)(128)(4,1)S(1)}, s32[]{:S(2)}) async-start(s8[6291456]{0:T(1024)(128)(4,1)} %bitcast.138), calls=%async_computation.3 | async-start | bytes 4194304
  245.6 4.9 copy-start.12
  250.4 2.3 copy-start.10
  259.7 3.0 copy-start.43
  260.5 2.2 copy-start.20
  268.6 5.9 copy-start.37
  268.6 5.9 copy-start.38
  708.8 12.1 %slice-start.2 = ((s8[9437184]{0:T(1024)(128)(4,1)}), s8[4194304]{0:T(1024)(128)(4,1)S(1)}, s32[]{:S(2)}) async-start(s8[9437184]{0:T(1024)(128)(4,1)} %bitcast.143), calls=%async_computation.4 | async-start | bytes 8388608
  712.1 8.8 %slice-start.3 = ((s8[9437184]{0:T(1024)(128)(4,1)}), s8[4194304]{0:T(1024)(128)(4,1)S(1)}, s32[]{:S(2)}) async-start(s8[9437184]{0:T(1024)(128)(4,1)} %bitcast.143), calls=%async_computation.5 | async-start | bytes 8388608
  712.1 8.8 %slice-start.4 = ((s8[9437184]{0:T(1024)(128)(4,1)}), s8[1048576]{0:T(1024)(128)(4,1)S(1)}, s32[]{:S(2)}) async-start(s8[9437184]{0:T(1024)(128)(4,1)} %bitcast.143), calls=%async_computation.6 | async-start | bytes 2097152
Sparse Core Ops, SparseCore 0:
  92.3 61.7 all-gather.1
  268.7 432.0 all-reduce.3
where the time goes:
time: 736 us; the launch traced here: 732 us
  waiting for transfers between devices  422 us (57%)
  matrix products  142 us (19%)
  local copies, waits for them, and re-layouts  77.2 us (10%)
  blocking collectives  41.7 us (6%)
  other arithmetic  34.4 us (5%)
  between operations  14.9 us (2%)
    psum x1, waiting for transfers between devices, on_device(): lax.psum((grad_w_qkv, grad_b_query, grad_b_value, grad_w_out, grad_b_out,...  376 us
    all_gather x1, waiting for transfers between devices, on_device(): everyone = lax.all_gather(pooled_low, ('tower', 'dp'), axis=0, tiled=True)  45.4 us
    psum x1, blocking collectives, on_device(): lax.psum((grad_w_qkv, grad_b_query, grad_b_value, grad_w_out, grad_b_out,...  41.7 us
    unnamed x134, local copies, waits for them, and re-layouts  40.9 us
    dot_general x1, matrix products, on_device(): up_rows = jnp.dot(hidden_low, w_in, preferred_element_type=f32) + b_in  35.3 us
    dot_general x1, matrix products, on_device(): jnp.einsum('nd,fd->nf', d_mid_low, w_down, preferred_element_type=f32)  19.2 us
  transfers between devices with their start and end apart: 2, of which 2 were waited for; matrix products, arithmetic and copies ran while one was open for 4% of the time, Pallas kernels for 0%

commit v1 on v0

--- a/solution.py
+++ b/solution.py
@@ -183,22 +183,25 @@
         grad_gain_two,
         grad_shift_two,
     ) = lax.psum(
-        (
-            grad_w_qkv,
-            grad_b_query,
-            grad_b_value,
-            grad_w_out,
-            grad_b_out,
-            grad_gain_one,
-            grad_shift_one,
-            grad_w_in,
-            grad_b_in,
-            grad_w_down,
-            grad_b_down,
-            grad_gain_two,
-            grad_shift_two,
+        lax.psum(
+            (
+                grad_w_qkv,
+                grad_b_query,
+                grad_b_value,
+                grad_w_out,
+                grad_b_out,
+                grad_gain_one,
+                grad_shift_one,
+                grad_w_in,
+                grad_b_in,
+                grad_w_down,
+                grad_b_down,
+                grad_gain_two,
+                grad_shift_two,
+            ),
+            "dp",
         ),
-        ("tower", "dp"),
+        "tower",
     )
     return (
         output_rows.astype(bf16)[None],

time: 736 us -> 1420 us (1.93)
  waiting for transfers between devices: 422 us -> 1080 us
  blocking collectives: 41.7 us -> 72.5 us
    psum x0 -> x1, waiting for transfers between devices: none -> 547 us  [on_device(): lax.psum(lax.psum((grad_w_qkv, grad_b_query, grad_b_value, grad_w_out, gr...]
    psum x1, waiting for transfers between devices: 376 us -> 486 us  [on_device(): lax.psum((grad_w_qkv, grad_b_query, grad_b_value, grad_w_out, grad_b_out,...]
    psum x1, blocking collectives: 41.7 us -> 61.7 us  [on_device(): lax.psum((grad_w_qkv, grad_b_query, grad_b_value, grad_w_out, grad_b_out,...]
  transfers between devices with their start and end apart: 2 -> 3, of which waited for: 2 -> 3; matrix products, arithmetic and copies ran while one was open for 4% -> 2% of each run, Pallas kernels for 0% -> 0%
where the time goes in v1:
time: 1420 us
  waiting for transfers between devices  1080 us (76%)
  matrix products  142 us (10%)
  local copies, waits for them, and re-layouts  77.1 us (5%)
  blocking collectives  72.5 us (5%)
  other arithmetic  34.2 us (2%)
  between operations  14.6 us (1%)
    psum x1, waiting for transfers between devices, on_device(): lax.psum(lax.psum((grad_w_qkv, grad_b_query, grad_b_value, grad_w_out, gr...  547 us
    psum x1, waiting for transfers between devices, on_device(): lax.psum((grad_w_qkv, grad_b_query, grad_b_value, grad_w_out, grad_b_out,...  486 us
    psum x1, blocking collectives, on_device(): lax.psum((grad_w_qkv, grad_b_query, grad_b_value, grad_w_out, grad_b_out,...  61.7 us
    all_gather x1, waiting for transfers between devices, on_device(): everyone = lax.all_gather(pooled_low, ('tower', 'dp'), axis=0, tiled=True)  45.4 us
    unnamed x134, local copies, waits for them, and re-layouts  40.8 us
    dot_general x1, matrix products, on_device(): up_rows = jnp.dot(hidden_low, w_in, preferred_element_type=f32) + b_in  35.3 us
  transfers between devices with their start and end apart: 3, of which 3 were waited for; matrix products, arithmetic and copies ran while one was open for 2% of the time, Pallas kernels for 0%

profile of v1, /device:TPU:0, one launch (start us, length us, event | category | flops | bytes accessed | tf_op | source)
XLA Modules:
  0.0 1418.5 jit_solution(10786900410841408086)
XLA Ops:
  7.2 1.5 convert_reduce_fusion
  8.8 1.6 broadcast_compare_fusion
  10.4 5.2 fusion.28
  15.6 1.3 slice.31
  16.9 2.3 fusion.11
  19.2 2.8 copy.45
  22.1 3.1 copy.70
  25.1 2.6 copy.47
  27.7 3.0 copy.72
  30.7 2.6 copy.46
  33.3 2.0 copy.71
  35.3 1.5 fusion.78
  36.9 1.6 fusion.6
  39.6 1.3 fusion.30
  40.9 1.2 copy.52
  42.6 1.7 fusion.79
  45.0 1.9 copy-done.28
  47.0 35.3 %multiply_convert_fusion = (bf16[1024,3072]{1,0:T(8,128)(2,1)S(1)}, f32[1024,3072]{1,0:T(8,128)}, f32[1024,3072]{1,0:T(8,128)}) fusion(f32[3072]{0:T(1024)S(1)} %copy-done.46, bf16[768,3072]{1,0:T(8,128)(2,1)S(1)} %bitcast.168, f32[1024,768]{1,0:T(8,128)S(1)} %get-tuple-element.99, f32[768]{0:T(1024)S(1)} %copy-done.34, f32[768]{0:T(1024)S(1)} %copy-done.28, ...), kind=kOutput, calls=%fused_computation.8 | convolution fusion | flops 5043388416 | bytes 39348224 | tf_op jit(solution)/shard_map/dot_general | solution.py:90
  82.3 5.4 fusion.80
  88.6 1.7 convert_bitcast_fusion
  90.4 1.8 fusion.44
  92.9 1.4 gather_fusion
  95.4 4.6 scatter_custom_fusion
  100.0 1.4 gather_fusion.1
  103.2 1.4 gather_fusion.3
  104.6 1.3 gather.24
  105.9 1.3 pad_clamp_fusion.1
  107.1 1.5 log_add_fusion
  108.7 45.4 %all-gather.2.cloned.1.call-done = bf16[2048,768]{1,0:T(8,128)(2,1)} async-done(((bf16[64,768]{1,0:T(8,128)(2,1)}), bf16[2048,768]{1,0:T(8,128)(2,1)}) %all-gather.2.cloned.1.call-update) | async-done | bytes 3145744 | tf_op jit(solution)/shard_map/all_gather | solution.py:110
  154.1 2.7 constant_dynamic-slice_fusion
  156.7 3.1 gather_fusion.2
  160.9 1.7 fusion.57
  163.0 1.3 rsqrt.49
  165.3 3.4 fusion.74
  168.7 1.5 fusion.12
  170.2 2.0 fusion.75
  172.2 7.7 fusion.47
  179.9 19.3 %fusion.81 = (f32[3072]{0:T(1024)}, bf16[1024,3072]{1,0:T(8,128)(2,1)}) fusion(f32[1024,3072]{1,0:T(8,128)} %get-tuple-element.88, bf16[3072,768]{1,0:T(8,128)(2,1)} %param.30, f32[1024,768]{1,0:T(8,128)} %copy-done.16, f32[1024,3072]{1,0:T(8,128)} %get-tuple-element.100, f32[3072]{0:T(1024)S(1)} %copy-done.47), kind=kOutput, calls=%fused_computation.162 | convolution fusion | flops 4882953216 | bytes 39346176 | tf_op jit(solution)/shard_map/nd,fd->nf/dot_general | solution.py:137
  199.2 11.6 multiply_reduce_fusion.1
  210.8 8.9 fusion.14
  219.7 1.8 fusion.76
  221.5 2.8 fusion.24
  224.3 2.6 convolution_convert_fusion
  226.9 2.6 copy.53
  229.5 1.9 copy.74
  231.4 6.9 bitcast_convert_fusion
  238.3 7.3 multiply_reduce_fusion
  245.6 4.9 multiply_convert_fusion.1
  250.5 2.3 fusion.31
  252.8 2.6 bitcast_convert_fusion.1
  256.6 1.2 copy.61
  260.4 2.1 copy-done.20
  262.6 5.8 convolution_bitcast_fusion
  268.4 486.1 %all-reduce.7.cloned.1.call-done = (f32[768,2304]{0,1:T(8,128)}, f32[768,768]{1,0:T(8,128)}, f32[768,3072]{1,0:T(8,128)}, f32[3072,768]{1,0:T(8,128)}) async-done(((f32[768,2304]{0,1:T(8,128)}, f32[768,768]{1,0:T(8,128)}, f32[768,3072]{1,0:T(8,128)}, f32[3072,768]{1,0:T(8,128)}), (f32[768,2304]{0,1:T(8,128)}, f32[768,768]{1,0:T(8,128)}, f32[768,3072]{1,0:T(8,128)}, ...) | async-done | bytes 28311568 | tf_op jit(solution)/shard_map/psum | solution.py:186
  754.6 2.1 bitcast_reduce_fusion
  757.4 2.2 bitcast_reduce_fusion.1
  760.3 61.7 %all-reduce = (f32[768]{0:T(1024)S(1)}, f32[768]{0:T(1024)S(1)}, f32[768]{0:T(1024)}, f32[768]{0:T(1024)}, f32[768]{0:T(1024)}, /*index=5*/f32[3072]{0:T(1024)}, f32[768]{0:T(1024)}, f32[768]{0:T(1024)}, f32[768]{0:T(1024)}) all-reduce(f32[768]{0:T(1024)} %reduce_sum.226, ...), channel_id=1, replica_groups=mesh['tower'=2,'dp'=16] {'dp'}, use_global_device_ids=true, to_apply=%region_19.20 | all-reduce | flops 9216 | bytes 73728 | tf_op jit(solution)/shard_map/psum | solution.py:186
  822.0 10.8 all-reduce.2
  832.8 8.5 add_bitcast_fusion
  841.3 546.7 %all-reduce.9.cloned.1.call-done = (f32[768,2304]{0,1:T(8,128)}, f32[768,768]{1,0:T(8,128)}, f32[768,3072]{1,0:T(8,128)}, f32[3072,768]{1,0:T(8,128)}) async-done(((f32[768,2304]{0,1:T(8,128)}, f32[768,768]{1,0:T(8,128)}, f32[768,3072]{1,0:T(8,128)}, f32[3072,768]{1,0:T(8,128)}), (f32[768,2304]{0,1:T(8,128)}, f32[768,768]{1,0:T(8,128)}, f32[768,3072]{1,0:T(8,128)}, ...) | async-done | bytes 28311568 | tf_op jit(solution)/shard_map/psum | solution.py:185
  1388.0 8.0 copy.65
  1395.9 3.4 copy.129
  1399.3 8.8 copy.130
  1408.1 3.7 copy.131
  (158 shorter events, 14.4 us)
Async XLA Ops:
  7.2 3.2 copy-start
  7.2 146.9 %all-gather.2.cloned.1.call-start = ((), (), s32[]{:S(2)}) async-start(), calls=%async_computation | async-start | bytes 3244032 | tf_op jit(solution)/shard_map/all_gather | solution.py:110
  15.6 1.3 copy-start.39
  15.6 1.3 copy-start.40
  33.3 2.0 copy-start.9
  33.3 2.0 copy-start.23
  35.3 1.5 copy-start.11
  36.8 2.7 copy-start.1
  36.9 2.7 copy-start.21
  36.9 2.7 copy-start.13
  38.5 2.3 copy-start.22
  40.9 1.4 copy-start.42
  40.9 1.7 copy-start.44
  40.9 1.7 copy-start.48
  42.1 2.2 copy-start.17
  42.1 2.9 slice-start.7
  42.6 2.4 slice-start.8
  42.6 39.7 %slice-start.5 = ((s8[4718592]{0:T(1024)(128)(4,1)}), s8[4194304]{0:T(1024)(128)(4,1)S(1)}, s32[]{:S(2)}) async-start(s8[4718592]{0:T(1024)(128)(4,1)} %bitcast.165), calls=%async_computation.8 | async-start | bytes 8388608
  44.3 38.0 %copy-start.6 = (f32[1024,768]{1,0:T(8,128)}, f32[1024,768]{1,0:T(8,128)S(1)}, u32[]{:S(2)}) copy-start(f32[1024,768]{1,0:T(8,128)S(1)} %get-tuple-element.99) | copy-start | bytes 9437188
  44.3 2.6 copy-start.28
  44.4 2.6 copy-start.34
  44.4 2.6 copy-start.46
  47.0 35.3 %slice-start.6 = ((s8[4718592]{0:T(1024)(128)(4,1)}), s8[524288]{0:T(1024)(128)(4,1)S(1)}, s32[]{:S(2)}) async-start(s8[4718592]{0:T(1024)(128)(4,1)} %bitcast.165), calls=%async_computation.9 | async-start | bytes 1048576
  47.0 35.3 %copy-start.49 = (f32[768]{0:T(1024)S(1)}, f32[768]{0:T(1024)}, u32[]{:S(2)}) copy-start(f32[768]{0:T(1024)} %param.31) | copy-start | bytes 9220
  82.3 5.5 copy-start.50
  87.8 2.5 copy-start.4
  87.8 0.8 copy-start.41
  87.8 2.5 copy-start.26
  88.6 1.8 copy-start.32
  88.6 1.8 copy-start.24
  88.6 1.8 copy-start.36
  90.3 2.5 copy-start.2
  90.3 12.9 copy-start.3
  92.2 662.4 %all-reduce.7.cloned.1.call-start = ((), (), s32[]{:S(2)}) async-start(), calls=%async_computation.1 | async-start | bytes 56623104 | tf_op jit(solution)/shard_map/psum | solution.py:186
  101.4 63.9 %copy-start.25 = (s32[1,8,128]{2,1,0:T(8,128)S(1)}, s32[1,8,128]{2,1,0:T(8,128)}, u32[]{:S(2)}) copy-start(s32[1,8,128]{2,1,0:T(8,128)} %param.18) | copy-start | bytes 12292
  108.7 60.0 %copy-start.27 = (f32[1024]{0:T(1024)S(1)}, f32[1024]{0:T(1024)}, u32[]{:S(2)}) copy-start(f32[1024]{0:T(1024)} %copy-done.26) | copy-start | bytes 12292
  164.4 4.3 copy-start.5
  164.4 4.3 copy-start.31
  164.4 4.3 copy-start.33
  168.7 3.6 slice-start.9
  170.2 2.0 slice-start.10
  172.2 7.7 copy-start.16
  172.2 7.7 copy-start.47
  179.9 19.3 %copy-start.29 = (f32[768]{0:T(1024)S(1)}, f32[768]{0:T(1024)}, u32[]{:S(2)}) copy-start(f32[768]{0:T(1024)} %param.26) | copy-start | bytes 9220
  199.2 11.6 copy-start.7
  199.2 11.6 copy-start.8
  199.2 11.6 copy-start.35
  219.7 1.8 copy-start.18
  221.5 2.8 copy-start.15
  221.5 2.8 copy-start.45
  229.5 1.9 copy-start.19
  231.4 6.9 copy-start.14
  231.4 14.2 %slice-start = ((s8[6291456]{0:T(1024)(128)(4,1)}), s8[4194304]{0:T(1024)(128)(4,1)S(1)}, s32[]{:S(2)}) async-start(s8[6291456]{0:T(1024)(128)(4,1)} %bitcast.138), calls=%async_computation.3 | async-start | bytes 8388608
  238.3 7.4 slice-start.1
  245.6 4.9 copy-start.12
  250.5 2.3 copy-start.10
  259.6 2.9 copy-start.43
  260.4 2.1 copy-start.20
  268.4 1119.6 %all-reduce.9.cloned.1.call-start = ((), (), s32[]{:S(2)}) async-start(), calls=%async_computation.2 | async-start | bytes 56623104 | tf_op jit(solution)/shard_map/psum | solution.py:185
  754.6 5.7 copy-start.37
  754.6 5.7 copy-start.38
  1395.9 12.1 slice-start.2
  1399.3 8.8 slice-start.3
  1399.3 8.8 slice-start.4
  (1 other events, 0.7 us)
Sparse Core Ops, SparseCore 0:
  92.3 61.7 all-gather.1
  268.5 486.0 all-reduce.6
  757.4 630.5 all-reduce.8
